TPU v7x, 128 devices: a whole 4x4x4 slice. The times are simulated.
128 devices in a mesh: row: 8 (over y, core), col: 16 (over z, x).
Axes of the slice: x: 4, y: 4, z: 4, core: 2. Of those that a mesh axis runs over, the one named last changes fastest.
Arguments:
- weight: bfloat16 [8192, 16384], P('row', 'col'), may hold values from -3 to 3
- momentum: float32 [8192, 16384], P('row', 'col'), may hold values from -100 to 100, as said below
- gradient: bfloat16 [8192, 16384], P('row', 'col'), may hold values from -6 to 6
- prev_basis: bfloat16 [16384, 512], P('col'), may hold values from -6 to 6
Outputs:
- new_weight: bfloat16 [8192, 16384], P('row', 'col')
- new_momentum: float32 [8192, 16384], P('row', 'col')
- new_basis: bfloat16 [16384, 512], P('col')
Inputs may be any that keep to these rules, and one draw needn't show every extreme that they name: momentum has rows and columns of different scales.
All inputs are finite; a program needn't handle non-finite values.
Results may differ from a plain program's by a relative error of at most 0.0021.
Values may be sent and summed in bfloat16 or wider, within the bound.
A program may use at most 128 MiB of HBM per device.

v0:
```python
import functools

import jax
import jax.numpy as jnp
from jax import lax
from jax.experimental import pallas as pl
from jax.experimental.pallas import tpu as pltpu
from jax.sharding import PartitionSpec as P

MESH = pl.DeviceIdType.MESH
F32 = jnp.float32
BF16 = jnp.bfloat16

M = 8192
N = 16384
R = 512
ROWS = 1024
COLS = 1024
NB = 128
SLICE = 128
SUB = 32

decay_loss = 0.1
step_size = 0.4
epsilon = 1e-06


def dims(a, b):
    return (((a,), (b,)), ((), ()))


def dot(a, b):
    return jnp.dot(a, b, preferred_element_type=F32)


def dot_t(a, b):
    return lax.dot_general(a, b, dims(0, 0), preferred_element_type=F32)


def dot_nt(a, b):
    return lax.dot_general(a, b, dims(1, 1), preferred_element_type=F32)


def split(x):
    high = x.astype(BF16)
    return high, (x - high.astype(F32)).astype(BF16)


def from_row(x, i):
    return jnp.broadcast_to(x[i : i + 1, :], x.shape)


def from_lane(x, k):
    return jnp.broadcast_to(x[:, k : k + 1], (8, NB))


HALF = NB // 16


def exact(a, b, contract):
    return lax.dot_general(
        a, b, contract, precision=lax.Precision.HIGHEST, preferred_element_type=F32
    )


def invert_leaf(z_ref):
    rows = lax.broadcasted_iota(jnp.int32, (8, NB), 0)
    lanes = lax.broadcasted_iota(jnp.int32, (8, NB), 1)
    tiles = [z_ref[8 * i : 8 * i + 8, :] for i in range(NB // 8)]
    for p in range(NB // 8):
        tile = tiles[p]
        columns = [from_lane(tile, 8 * p + k) for k in range(8)]
        own = (lanes >= 8 * p) & (lanes < 8 * p + 8)
        tile = jnp.where(own, jnp.where(lanes - 8 * p == rows, 1.0, 0.0), tile)
        below = tiles[p + 1 : (p // HALF + 1) * HALF]
        near = [from_lane(below[0], 8 * p + k) for k in range(8)] if below else None
        upper, factors = [], []
        for j in range(8):
            inverse = lax.rsqrt(from_row(columns[j], j))
            t = columns[j] * inverse
            masked = jnp.where(rows > j, t, 0.0)
            u = from_row(tile, j) * inverse
            upper.append(u)
            tile = jnp.where(rows == j, u, tile - masked * u)
            if near:
                factors.append(near[j] * inverse)
            for k in range(j + 1, 8):
                tk = from_row(t, k)
                columns[k] = columns[k] - masked * tk
                if near:
                    near[k] = near[k] - factors[j] * tk
        tiles[p] = tile

        def eliminated(x, factors):
            terms = [t * u for t, u in zip(factors, upper)]
            while len(terms) > 1:
                terms = [terms[i] + terms[i + 1] for i in range(0, len(terms), 2)]
            return jnp.where(own, 0.0, x) - terms[0]

        if below:
            tiles[p + 1] = eliminated(below[0], factors)
        if len(below) > 1:
            turned = tile.T
            for i in range(p + 2, p + 1 + len(below)):
                part = turned[8 * i : 8 * i + 8, :]
                tiles[i] = eliminated(tiles[i], [from_lane(part, k) for k in range(8)])
        if p == HALF - 1:
            done = jnp.concatenate(tiles[:HALF], axis=0)
            row = lax.broadcasted_iota(jnp.int32, done.shape, 0)
            lane = lax.broadcasted_iota(jnp.int32, done.shape, 1)
            inside = lane < 8 * HALF
            rest = jnp.concatenate(tiles[HALF:], axis=0)
            rest = jnp.where(inside, 0.0, rest) - exact(
                done[:, 8 * HALF :], jnp.where(inside & (lane > row), 0.0, done), dims(0, 0)
            )
            tiles[HALF:] = [rest[8 * i : 8 * i + 8, :] for i in range(HALF)]
    for i in range(NB // 8):
        z_ref[8 * i : 8 * i + 8, :] = tiles[i]


def invert_cholesky(z_ref, d_ref, between):
    lower = lax.broadcasted_iota(jnp.int32, (NB, NB), 0) >= lax.broadcasted_iota(
        jnp.int32, (NB, NB), 1
    )
    for b in range(R // NB):
        lo, hi = b * NB, (b + 1) * NB
        d_ref[...] = z_ref[lo:hi, lo:hi]
        invert_leaf(d_ref)
        block = jnp.where(lower, d_ref[...], 0.0)
        z_ref[lo:hi, lo:hi] = block
        if b:
            z_ref[lo:hi, :lo] = exact(block, z_ref[lo:hi, :lo], dims(1, 0))
        if hi < R:
            upper = exact(block, z_ref[lo:hi, hi:], dims(1, 0))
            z_ref[lo:hi, hi:] = upper
            z_ref[hi:, lo:hi] = jnp.zeros((R - hi, NB), F32)
            z_ref[hi:, :] -= exact(upper, z_ref[lo:hi, :], dims(0, 0))
            z_ref[lo:hi, hi:] = jnp.zeros((NB, R - hi), F32)
        between(b)


class Copies:
    def __init__(self, send_sems, recv_sems):
        self.send_sems, self.recv_sems = send_sems, recv_sems
        self.count = 0
        self.unfinished = []

    def start(self, src, dst, device):
        i = self.count
        self.count += 1
        copy = pltpu.make_async_remote_copy(
            src_ref=src,
            dst_ref=dst,
            send_sem=self.send_sems.at[i],
            recv_sem=self.recv_sems.at[i],
            device_id=device,
            device_id_type=MESH,
        )
        copy.start()
        self.unfinished.append(copy)
        return copy

    def finish(self):
        for copy in self.unfinished:
            copy.wait_send()


class Ring:
    def __init__(self, copies, place, right, left, columns=slice(None)):
        self.copies, self.place, self.right, self.left = copies, place, right, left
        self.columns = columns

    def rows(self, base, size, ahead, part=None):
        start = base + size * lax.rem(self.place + ahead, 4)
        if part is None:
            return pl.ds(pl.multiple_of(start, 8), size)
        return pl.ds(pl.multiple_of(start + part * (size // 2), 8), size // 2)

    def scatter_far(self, src, base, size, far, near):
        self.src, self.base, self.size, self.far, self.near = src, base, size, far, near
        start, cols = self.copies.start, self.columns
        self.far_right = start(
            src.at[self.rows(base, size, 2, 0), cols], far.at[0, :, cols], self.right
        )
        self.far_left = start(
            src.at[self.rows(base, size, 2, 1), cols], far.at[1, :, cols], self.left
        )

    def scatter_near(self):
        src, base, size, near, cols = self.src, self.base, self.size, self.near, self.columns
        half = size // 2
        self.near_right = self.copies.start(
            src.at[self.rows(base, size, 1, 1), cols], near.at[0, half:, cols], self.right
        )
        self.near_left = self.copies.start(
            src.at[self.rows(base, size, 3, 0), cols], near.at[1, :half, cols], self.left
        )

    def scatter_start(self, *args):
        self.scatter_far(*args)
        self.scatter_near()

    def scatter_middle(self):
        half, cols = self.size // 2, self.columns
        self.far_right.wait_recv()
        rows = self.rows(self.base, self.size, 1, 0)
        self.src[rows, cols] += self.far[0, :, cols]
        self.last_right = self.copies.start(
            self.src.at[rows, cols], self.near.at[0, :half, cols], self.right
        )
        self.far_left.wait_recv()
        rows = self.rows(self.base, self.size, 3, 1)
        self.src[rows, cols] += self.far[1, :, cols]
        self.last_left = self.copies.start(
            self.src.at[rows, cols], self.near.at[1, half:, cols], self.left
        )

    def scatter_end(self, out, out_rows):
        cols = self.columns
        for copy in (self.near_right, self.near_left, self.last_right, self.last_left):
            copy.wait_recv()
        own = self.src[self.rows(self.base, self.size, 0), cols]
        out[out_rows, cols] = own + self.near[0, :, cols] + self.near[1, :, cols]

    def gather_start(self, buf, base, size):
        self.buf, self.base, self.size = buf, base, size
        own = buf.at[self.rows(base, size, 0), self.columns]
        self.to_right = self.copies.start(own, own, self.right)
        self.to_left = self.copies.start(own, own, self.left)

    def gather_middle(self):
        self.to_right.wait_recv()
        part = self.buf.at[self.rows(self.base, self.size, 3, 0), self.columns]
        self.on_right = self.copies.start(part, part, self.right)
        self.to_left.wait_recv()
        part = self.buf.at[self.rows(self.base, self.size, 1, 1), self.columns]
        self.on_left = self.copies.start(part, part, self.left)

    def gather_end(self):
        self.on_right.wait_recv()
        self.on_left.wait_recv()


BLOCKS = [(i, j) for i in range(R // NB) for j in range(i, R // NB)]
PACKED = len(BLOCKS) * NB
LIMIT = 42 * 1024 * 1024
COPIES = 128
CHUNKS = [slice(0, R // 2), slice(R // 2, R)]


def kernel(
    momentum, gradient, weight, basis,
    right_out, scaled_out, high_out, low_out, buffer_out, weight_out,
    mom, grad, prev, high, low, high_t, low_t,
    part, first_a, first_b, left, far_x, near_x, far_z, near_z, far_x2, near_x2, far_z2, near_z2,
    gram, packed, packed_in, packed_sum, gram_far, gram_near,
    right, right_in, right_sum, right_far, right_near,
    tri, block, tri_h, tri_l, squares,
    load_sems, send_sems, recv_sems,
):
    r, c = lax.axis_index("row"), lax.axis_index("col")
    y, core = r // 2, lax.rem(r, 2)
    z, x = c // 4, lax.rem(c, 4)

    def at(dy=0, dz=0, dx=0):
        return (
            lax.rem(y + dy, 4) * 2 + core,
            lax.rem(z + dz, 4) * 4 + lax.rem(x + dx, 4),
        )

    sibling = (y * 2 + 1 - core, c)

    order = []
    for ahead in (2, 1, 3, 0):
        order.append(lax.rem(x + ahead, 4) * SLICE)
        order.append(ROWS // 2 + lax.rem(z + ahead, 4) * SLICE)
    order = [pl.ds(pl.multiple_of(start, SLICE), SLICE) for start in order]
    load_basis = pltpu.make_async_copy(basis, prev, load_sems.at[16])
    load_basis.start()
    loads = []
    for i, rows in enumerate(order):
        a = pltpu.make_async_copy(momentum.at[rows], mom.at[rows], load_sems.at[2 * i])
        b = pltpu.make_async_copy(gradient.at[rows], grad.at[rows], load_sems.at[2 * i + 1])
        a.start()
        b.start()
        loads.append((a, b))

    barrier = pltpu.get_barrier_semaphore()
    peers = [sibling, at(dy=1), at(dy=3)] + [(r, lax.rem(c + k, 16)) for k in range(1, 16)]
    for peer in peers:
        pl.semaphore_signal(barrier, inc=1, device_id=peer, device_id_type=MESH)

    copies = Copies(send_sems, recv_sems)
    x_ring = lambda cols: Ring(copies, x, at(dx=1), at(dx=3), cols)
    z_ring = lambda cols: Ring(copies, z, at(dz=1), at(dz=3), cols)
    outer = [(x_ring(cols), z_ring(cols)) for cols in CHUNKS]
    inner = [(z_ring(cols), x_ring(cols)) for cols in CHUNKS]
    ring_g = Ring(copies, y, at(dy=1), at(dy=3))
    ring_w = Ring(copies, y, at(dy=1), at(dy=3))

    def partial_left(i):
        rows = order[i]
        for load in loads[i]:
            load.wait()
        buffer = mom[rows, :] + grad[rows, :].astype(F32)
        buffer_out[rows, :] = buffer
        h, l = split(buffer)
        high[rows, :] = h
        low[rows, :] = l
        both = dot(jnp.concatenate([h, l], axis=0), prev[...])
        part[rows, :] = both[:SLICE] + both[SLICE:]

    load_basis.wait()
    for i in range(2):
        partial_left(i)
    pl.semaphore_wait(barrier, len(peers))
    for a, b in outer:
        a.scatter_far(part, 0, SLICE, far_x, near_x)
        b.scatter_far(part, ROWS // 2, SLICE, far_z, near_z)
    for i in range(2, 6):
        partial_left(i)
    for a, b in outer:
        a.scatter_near()
        b.scatter_near()
    for i in range(6, 8):
        partial_left(i)
    for a, b in outer:
        a.scatter_middle()
        b.scatter_middle()

    load_weight = pltpu.make_async_copy(weight, weight_out, load_sems.at[17])
    load_weight.start()

    @pl.loop(0, ROWS // NB)
    def _(k):
        rows = pl.ds(pl.multiple_of(k * NB, NB), NB)
        high_t[:, rows] = high[rows, :].T
        low_t[:, rows] = low[rows, :].T

    everything = pl.ds(0, SLICE)
    for (a, b), (a2, b2) in zip(outer, inner):
        a.scatter_end(first_a, everything)
        a2.scatter_start(first_a, 0, SUB, far_z2, near_z2)
        b.scatter_end(first_b, everything)
        b2.scatter_start(first_b, 0, SUB, far_x2, near_x2)
    for a2, b2 in inner:
        a2.scatter_middle()
        b2.scatter_middle()
    base_a = x * SLICE
    base_b = ROWS // 2 + z * SLICE
    for a2, b2 in inner:
        a2.scatter_end(left, a2.rows(base_a, SUB, 0))
        a2.gather_start(left, base_a, SUB)
        b2.scatter_end(left, b2.rows(base_b, SUB, 0))
        b2.gather_start(left, base_b, SUB)
    for a2, b2 in inner:
        a2.gather_middle()
        b2.gather_middle()
    for (a, b), (a2, b2) in zip(outer, inner):
        a2.gather_end()
        a.gather_start(left, 0, SLICE)
        b2.gather_end()
        b.gather_start(left, ROWS // 2, SLICE)

    def slices(ahead):
        return (
            pl.ds(pl.multiple_of(lax.rem(x + ahead, 4) * SLICE, SLICE), SLICE),
            pl.ds(pl.multiple_of(ROWS // 2 + lax.rem(z + ahead, 4) * SLICE, SLICE), SLICE),
        )

    def halves(ahead):
        a, b = slices(ahead)
        return split(jnp.concatenate([left[a, :], left[b, :]], axis=0))

    def add_gram(ahead, first):
        h, l = halves(ahead)
        for i in range(R // NB):
            lo, hi = i * NB, (i + 1) * NB
            hl, ll = h[:, lo:hi], l[:, lo:hi]
            term = dot_t(hl, h[:, lo:]) + (
                dot_t(hl, l[:, lo:]) + dot_t(ll, h[:, lo:]) + dot_t(ll, l[:, lo:])
            )
            if first:
                gram[lo:hi, lo:] = term
            else:
                gram[lo:hi, lo:] += term

    def add_right(ahead, first):
        a, b = slices(ahead)
        h, l = halves(ahead)

        @pl.loop(0, COLS // 256)
        def _(k):
            rows = pl.ds(pl.multiple_of(k * 256, 256), 256)
            bh = jnp.concatenate([high_t[rows, a], high_t[rows, b]], axis=1)
            bl = jnp.concatenate([low_t[rows, a], low_t[rows, b]], axis=1)
            both = dot(jnp.concatenate([bh, bl], axis=0), h)
            term = both[:256] + (dot(bh, l) + both[256:])
            if first:
                right[rows, :] = term
            else:
                right[rows, :] += term

    add_gram(0, True)
    add_right(0, True)
    for a, b in outer:
        a.gather_middle()
        b.gather_middle()
    add_gram(1, False)
    add_gram(3, False)
    add_right(1, False)
    add_right(3, False)
    for a, b in outer:
        a.gather_end()
        b.gather_end()
    add_gram(2, False)

    for k, (i, j) in enumerate(BLOCKS):
        packed[k * NB : (k + 1) * NB, :] = gram[i * NB : (i + 1) * NB, j * NB : (j + 1) * NB]

    def half_of(whole, which):
        return pl.ds(pl.multiple_of(which * (whole // 2), 8), whole // 2)

    mine_g, other_g = half_of(PACKED, core), half_of(PACKED, 1 - core)
    mine_w, other_w = half_of(COLS, core), half_of(COLS, 1 - core)
    swap_g = copies.start(packed.at[other_g], packed_in, sibling)
    add_right(2, False)
    swap_w = copies.start(right.at[other_w], right_in, sibling)
    swap_g.wait_recv()
    packed[mine_g, :] += packed_in[...]
    ring_g.scatter_start(packed, core * (PACKED // 2), PACKED // 8, gram_far, gram_near)
    ring_g.scatter_middle()
    swap_w.wait_recv()
    right[mine_w, :] += right_in[...]
    ring_w.scatter_far(right, core * (COLS // 2), COLS // 8, right_far, right_near)
    ring_g.scatter_end(packed_sum, ring_g.rows(core * (PACKED // 2), PACKED // 8, 0))
    ring_g.gather_start(packed_sum, core * (PACKED // 2), PACKED // 8)
    ring_w.scatter_near()
    ring_g.gather_middle()
    ring_g.gather_end()
    back_g = copies.start(packed_sum.at[mine_g], packed_sum.at[mine_g], sibling)
    ring_w.scatter_middle()
    back_g.wait_recv()
    for k, (i, j) in enumerate(BLOCKS):
        tri[i * NB : (i + 1) * NB, j * NB : (j + 1) * NB] = packed_sum[k * NB : (k + 1) * NB, :]

    swaps = []

    def between(b):
        if b == 0:
            ring_w.scatter_end(right_sum, ring_w.rows(core * (COLS // 2), COLS // 8, 0))
            ring_w.gather_start(right_sum, core * (COLS // 2), COLS // 8)
        elif b == 1:
            ring_w.gather_middle()
        elif b == 2:
            ring_w.gather_end()
            swaps.append(
                copies.start(right_sum.at[mine_w], right_sum.at[mine_w], sibling)
            )

    invert_cholesky(tri, block, between)
    swaps[0].wait_recv()

    tri_h[...], tri_l[...] = split(tri[...].T)
    squares[c] = jnp.zeros((8, R), F32)
    h2 = R // 2

    def solved(value):
        h, l = split(value)
        n = len(value)
        both = jnp.concatenate([h, l], axis=0)
        halves = []
        for width, out in ((h2, slice(0, h2)), (R, slice(h2, R))):
            p = dot(both[:, :width], tri_h[:width, out])
            q = dot(h[:, :width], tri_l[:width, out])
            halves.append(p[:n] + (p[n:] + q))
        return jnp.concatenate(halves, axis=1)

    @pl.loop(0, COLS // 256)
    def _(k):
        rows = pl.ds(pl.multiple_of(k * 256, 256), 256)
        value = solved(right_sum[rows, :])
        mom[rows, R:] = value
        squares[c] += jnp.sum((value * value).reshape(32, 8, R), axis=0)

    sums = []
    for k in range(1, 16):
        sums.append(copies.start(squares.at[c], squares.at[c], (r, lax.rem(c + k, 16))))

    @pl.loop(0, ROWS // 256)
    def _(k):
        rows = pl.ds(pl.multiple_of(k * 256, 256), 256)
        value = solved(left[rows, :])
        mom[rows, :R] = value
        h, l = split(value)
        high_out[rows, :] = h
        low_out[rows, :] = l

    for copy in sums:
        copy.wait_recv()
    total = squares[0]
    for k in range(1, 16):
        total = total + squares[k]
    total = jnp.sum(total, axis=0, keepdims=True)
    scale = jnp.sqrt(total / N + epsilon)
    inverse = 1.0 / scale
    right_out[...] = (mom[:, R:] * inverse).astype(BF16)
    scaled_out[...] = (mom[:, :R] * scale).astype(BF16)
    load_weight.wait()
    copies.finish()


def factors(momentum, gradient, weight, basis):
    vmem = pl.BlockSpec(memory_space=pltpu.VMEM)
    any_ = pl.BlockSpec(memory_space=pltpu.HBM)
    f = lambda *s: pltpu.VMEM(s, F32)
    b = lambda *s: pltpu.VMEM(s, BF16)
    ring = lambda s, w: [f(2, s // 2, w), f(2, s, w)]
    return pl.pallas_call(
        kernel,
        out_shape=[
            jax.ShapeDtypeStruct((COLS, R), BF16),
            jax.ShapeDtypeStruct((ROWS, R), BF16),
            jax.ShapeDtypeStruct((ROWS, R), BF16),
            jax.ShapeDtypeStruct((ROWS, R), BF16),
            jax.ShapeDtypeStruct((ROWS, COLS), F32),
            jax.ShapeDtypeStruct((ROWS, COLS), BF16),
        ],
        in_specs=[any_] * 4,
        out_specs=[vmem] * 6,
        scratch_shapes=[
            f(ROWS, COLS), b(ROWS, COLS), b(COLS, R),
            b(ROWS, COLS), b(ROWS, COLS), b(COLS, ROWS), b(COLS, ROWS),
            f(ROWS, R), f(SLICE, R), f(SLICE, R), f(ROWS, R),
            *ring(SLICE, R), *ring(SLICE, R), *ring(SUB, R), *ring(SUB, R),
            f(R, R), f(PACKED, NB), f(PACKED // 2, NB), f(PACKED, NB), *ring(PACKED // 8, NB),
            f(COLS, R), f(COLS // 2, R), f(COLS, R), *ring(COLS // 8, R),
            f(R, R), f(NB, NB), b(R, R), b(R, R), f(16, 8, R),
            pltpu.SemaphoreType.DMA((18,)),
            pltpu.SemaphoreType.DMA((COPIES,)),
            pltpu.SemaphoreType.DMA((COPIES,)),
        ],
        compiler_params=pltpu.CompilerParams(
            collective_id=0, has_side_effects=True, vmem_limit_bytes=LIMIT
        ),
        name="factors",
    )(momentum, gradient, weight, basis)


def last_kernel(b, w, scaled, high, low, v, basis, new_w, new_m, new_v):
    buffer = b[...]
    vs = v[...]
    rows = len(buffer)
    both = dot_nt(jnp.concatenate([scaled[...], high[...], low[...]], axis=0), vs)
    new_m[...] = buffer - decay_loss * both[:rows]
    update = both[rows : 2 * rows] + both[2 * rows :]
    rate = step_size * (M / N) ** 0.5
    new_w[...] = (w[...].astype(F32) - rate * update).astype(BF16)
    new_v[...] = basis[...]


def outputs(buffer, weight, scaled, high, low, v):
    rows = 256
    wide = pl.BlockSpec((rows, COLS), lambda i: (i, 0))
    thin = pl.BlockSpec((rows, R), lambda i: (i, 0))
    whole = pl.BlockSpec((COLS, R), lambda i: (0, 0))
    return pl.pallas_call(
        last_kernel,
        grid=(ROWS // rows,),
        out_shape=[
            jax.ShapeDtypeStruct((ROWS, COLS), BF16),
            jax.ShapeDtypeStruct((ROWS, COLS), F32),
            jax.ShapeDtypeStruct((COLS, R), BF16),
        ],
        in_specs=[wide, wide, thin, thin, thin, whole, thin],
        out_specs=[wide, wide, thin],
        compiler_params=pltpu.CompilerParams(vmem_limit_bytes=20 * 1024 * 1024),
        name="outputs",
    )(buffer, weight, scaled, high, low, v, v)


def per_device(weight, momentum, gradient, prev_basis):
    kept = [
        pltpu.with_memory_space_constraint(a, pltpu.HBM)
        for a in (momentum, gradient, weight, prev_basis)
    ]
    v, *rest, buffer, held = factors(*kept)
    return tuple(outputs(buffer, held, *rest, v))


def solution(mesh):
    return jax.shard_map(
        per_device,
        mesh=mesh,
        in_specs=(P("row", "col"), P("row", "col"), P("row", "col"), P("col", None)),
        out_specs=(P("row", "col"), P("row", "col"), P("col", None)),
        check_vma=False,
    )
```

profile of v0, /device:TPU:1, one launch (start us, length us, event | category | flops | bytes accessed | tf_op | source)
XLA Modules:
  0.0 102.0 jit_solution(15818407085158499598)
XLA Ops:
  0.6 96.1 %factors.1 = (bf16[1024,512]{1,0:T(8,128)(2,1)S(1)}, bf16[1024,512]{1,0:T(8,128)(2,1)S(1)}, bf16[1024,512]{1,0:T(8,128)(2,1)S(1)}, bf16[1024,512]{1,0:T(8,128)(2...) custom-call(f32[1024,1024]{1,0:T(8,128)} %momentum.1, bf16[1024,1024]{1,0:T(8,128)(2,1)} %gradient.1, ...), custom_call_target="tpu_custom_call" | custom-call | tf_op jit(solution)/shard_map/factors/pallas_call | solution.py:519
  96.8 5.2 %outputs.1 = (bf16[1024,1024]{1,0:T(8,128)(2,1)}, f32[1024,1024]{1,0:T(8,128)}, bf16[1024,512]{1,0:T(8,128)(2,1)}) custom-call(f32[1024,1024]{1,0:T(8,128)S(1)} %get-tuple-element.9.b, bf16[1024,1024]{1,0:T(8,128)(2,1)S(1)} %get-tuple-element.10.w, bf16[1024,512]{1,0:T(8,128)(2,1)S(1)} %get-tuple-element.11.scaled, ...), custom_call_target="tpu_custom_call" | custom-call | tf_op jit(solution)/shard_map/outputs/pallas_call | solution.py:567
where the time goes:
time: 102 us
  Pallas kernels  101 us (99%)
    pallas_call x1, Pallas kernels, factors(): pl.pallas_call(kernel, out_shape=[jax.ShapeDtypeStruct((COLS, R), BF16),...  96.1 us
    pallas_call x1, Pallas kernels, outputs(): pl.pallas_call(last_kernel, grid=(ROWS // rows,), out_shape=[jax.ShapeDty...  5.23 us

commit v1 on v0

--- a/solution.py
+++ b/solution.py
@@ -63,7 +63,7 @@
     )
 
 
-def invert_leaf(z_ref):
+def invert_leaf(z_ref, between):
     rows = lax.broadcasted_iota(jnp.int32, (8, NB), 0)
     lanes = lax.broadcasted_iota(jnp.int32, (8, NB), 1)
     tiles = [z_ref[8 * i : 8 * i + 8, :] for i in range(NB // 8)]
@@ -105,6 +105,7 @@
                 part = turned[8 * i : 8 * i + 8, :]
                 tiles[i] = eliminated(tiles[i], [from_lane(part, k) for k in range(8)])
         if p == HALF - 1:
+            between()
             done = jnp.concatenate(tiles[:HALF], axis=0)
             row = lax.broadcasted_iota(jnp.int32, done.shape, 0)
             lane = lax.broadcasted_iota(jnp.int32, done.shape, 1)
@@ -125,7 +126,7 @@
     for b in range(R // NB):
         lo, hi = b * NB, (b + 1) * NB
         d_ref[...] = z_ref[lo:hi, lo:hi]
-        invert_leaf(d_ref)
+        invert_leaf(d_ref, lambda: between(2 * b))
         block = jnp.where(lower, d_ref[...], 0.0)
         z_ref[lo:hi, lo:hi] = block
         if b:
@@ -136,7 +137,7 @@
             z_ref[hi:, lo:hi] = jnp.zeros((R - hi, NB), F32)
             z_ref[hi:, :] -= exact(upper, z_ref[lo:hi, :], dims(0, 0))
             z_ref[lo:hi, hi:] = jnp.zeros((NB, R - hi), F32)
-        between(b)
+        between(2 * b + 1)
 
 
 class Copies:
@@ -244,7 +245,8 @@
 BLOCKS = [(i, j) for i in range(R // NB) for j in range(i, R // NB)]
 PACKED = len(BLOCKS) * NB
 LIMIT = 42 * 1024 * 1024
-COPIES = 128
+COPIES = 160
+PIECE = PACKED // 32
 CHUNKS = [slice(0, R // 2), slice(R // 2, R)]
 
 
@@ -253,7 +255,7 @@
     right_out, scaled_out, high_out, low_out, buffer_out, weight_out,
     mom, grad, prev, high, low, high_t, low_t,
     part, first_a, first_b, left, far_x, near_x, far_z, near_z, far_x2, near_x2, far_z2, near_z2,
-    gram, packed, packed_in, packed_sum, gram_far, gram_near,
+    gram, packed, packed_sum, gram_in, gram_y,
     right, right_in, right_sum, right_far, right_near,
     tri, block, tri_h, tri_l, squares,
     load_sems, send_sems, recv_sems,
@@ -286,7 +288,7 @@
         loads.append((a, b))
 
     barrier = pltpu.get_barrier_semaphore()
-    peers = [sibling, at(dy=1), at(dy=3)] + [(r, lax.rem(c + k, 16)) for k in range(1, 16)]
+    peers = [sibling, at(dy=1), at(dy=2), at(dy=3)] + [(r, lax.rem(c + k, 16)) for k in range(1, 16)]
     for peer in peers:
         pl.semaphore_signal(barrier, inc=1, device_id=peer, device_id_type=MESH)
 
@@ -295,8 +297,7 @@
     z_ring = lambda cols: Ring(copies, z, at(dz=1), at(dz=3), cols)
     outer = [(x_ring(cols), z_ring(cols)) for cols in CHUNKS]
     inner = [(z_ring(cols), x_ring(cols)) for cols in CHUNKS]
-    ring_g = Ring(copies, y, at(dy=1), at(dy=3))
-    ring_w = Ring(copies, y, at(dy=1), at(dy=3))
+    rings_w = [Ring(copies, y, at(dy=1), at(dy=3), cols) for cols in CHUNKS]
 
     def partial_left(i):
         rows = order[i]
@@ -421,45 +422,61 @@
     def half_of(whole, which):
         return pl.ds(pl.multiple_of(which * (whole // 2), 8), whole // 2)
 
-    mine_g, other_g = half_of(PACKED, core), half_of(PACKED, 1 - core)
+    mine_g = half_of(PACKED, core)
     mine_w, other_w = half_of(COLS, core), half_of(COLS, 1 - core)
-    swap_g = copies.start(packed.at[other_g], packed_in, sibling)
+
+    def piece(which, of):
+        return pl.ds(pl.multiple_of(which * (PACKED // 2) + of * PIECE, 8), PIECE)
+
+    swap_g = copies.start(packed.at[piece(1 - core, c)], gram_in, sibling)
     add_right(2, False)
-    swap_w = copies.start(right.at[other_w], right_in, sibling)
+    swaps_w = [
+        copies.start(right.at[other_w, cols], right_in.at[:, cols], sibling)
+        for cols in CHUNKS
+    ]
     swap_g.wait_recv()
-    packed[mine_g, :] += packed_in[...]
-    ring_g.scatter_start(packed, core * (PACKED // 2), PACKED // 8, gram_far, gram_near)
-    ring_g.scatter_middle()
-    swap_w.wait_recv()
-    right[mine_w, :] += right_in[...]
-    ring_w.scatter_far(right, core * (COLS // 2), COLS // 8, right_far, right_near)
-    ring_g.scatter_end(packed_sum, ring_g.rows(core * (PACKED // 2), PACKED // 8, 0))
-    ring_g.gather_start(packed_sum, core * (PACKED // 2), PACKED // 8)
-    ring_w.scatter_near()
-    ring_g.gather_middle()
-    ring_g.gather_end()
+    gram_y[y] = packed[piece(core, c), :] + gram_in[...]
+    over_y = [copies.start(gram_y.at[y], gram_y.at[y], at(dy=k)) for k in (2, 1, 3)]
+    for cols, swap, ring in zip(CHUNKS, swaps_w, rings_w):
+        swap.wait_recv()
+        right[mine_w, cols] += right_in[:, cols]
+        ring.scatter_far(right, core * (COLS // 2), COLS // 8, right_far, right_near)
+    for copy in over_y:
+        copy.wait_recv()
+    own_piece = packed_sum.at[piece(core, c)]
+    own_piece[...] = (gram_y[0] + gram_y[1]) + (gram_y[2] + gram_y[3])
+    over_col = [
+        copies.start(own_piece, own_piece, (r, lax.rem(c + k, 16))) for k in range(1, 16)
+    ]
+    for ring in rings_w:
+        ring.scatter_near()
+    for ring in rings_w:
+        ring.scatter_middle()
+    for copy in over_col:
+        copy.wait_recv()
     back_g = copies.start(packed_sum.at[mine_g], packed_sum.at[mine_g], sibling)
-    ring_w.scatter_middle()
     back_g.wait_recv()
     for k, (i, j) in enumerate(BLOCKS):
         tri[i * NB : (i + 1) * NB, j * NB : (j + 1) * NB] = packed_sum[k * NB : (k + 1) * NB, :]
 
     swaps = []
 
-    def between(b):
-        if b == 0:
-            ring_w.scatter_end(right_sum, ring_w.rows(core * (COLS // 2), COLS // 8, 0))
-            ring_w.gather_start(right_sum, core * (COLS // 2), COLS // 8)
-        elif b == 1:
-            ring_w.gather_middle()
-        elif b == 2:
-            ring_w.gather_end()
-            swaps.append(
-                copies.start(right_sum.at[mine_w], right_sum.at[mine_w], sibling)
-            )
+    def between(step):
+        if step == 0:
+            for ring in rings_w:
+                ring.scatter_end(right_sum, ring.rows(core * (COLS // 2), COLS // 8, 0))
+                ring.gather_start(right_sum, core * (COLS // 2), COLS // 8)
+        elif step in (2, 4):
+            rings_w[step // 2 - 1].gather_middle()
+        elif step in (5, 6):
+            ring = rings_w[step - 5]
+            ring.gather_end()
+            own = right_sum.at[mine_w, ring.columns]
+            swaps.append(copies.start(own, own, sibling))
 
     invert_cholesky(tri, block, between)
-    swaps[0].wait_recv()
+    for swap in swaps:
+        swap.wait_recv()
 
     tri_h[...], tri_l[...] = split(tri[...].T)
     squares[c] = jnp.zeros((8, R), F32)
@@ -533,7 +550,7 @@
             b(ROWS, COLS), b(ROWS, COLS), b(COLS, ROWS), b(COLS, ROWS),
             f(ROWS, R), f(SLICE, R), f(SLICE, R), f(ROWS, R),
             *ring(SLICE, R), *ring(SLICE, R), *ring(SUB, R), *ring(SUB, R),
-            f(R, R), f(PACKED, NB), f(PACKED // 2, NB), f(PACKED, NB), *ring(PACKED // 8, NB),
+            f(R, R), f(PACKED, NB), f(PACKED, NB), f(PIECE, NB), f(4, PIECE, NB),
             f(COLS, R), f(COLS // 2, R), f(COLS, R), *ring(COLS // 8, R),
             f(R, R), f(NB, NB), b(R, R), b(R, R), f(16, 8, R),
             pltpu.SemaphoreType.DMA((18,)),

time: 102 us -> 94 us (0.922)
  Pallas kernels: 101 us -> 93.3 us
    pallas_call x1, Pallas kernels: 96.1 us -> 88.1 us  [factors(): pl.pallas_call(kernel, out_shape=[jax.ShapeDtypeStruct((COLS, R), BF16),...]
where the time goes in v1:
time: 94 us; the launch traced here: 93.9 us
  Pallas kernels  93.3 us (99%)
    pallas_call x1, Pallas kernels, factors(): pl.pallas_call(kernel, out_shape=[jax.ShapeDtypeStruct((COLS, R), BF16),...  88.1 us
    pallas_call x1, Pallas kernels, outputs(): pl.pallas_call(last_kernel, grid=(ROWS // rows,), out_shape=[jax.ShapeDty...  5.23 us

profile of v1, /device:TPU:1, one launch (start us, length us, event | category | flops | bytes accessed | tf_op | source)
XLA Modules:
  0.0 93.9 jit_solution(11593867165964880755)
XLA Ops:
  0.6 88.1 %factors.1 = (bf16[1024,512]{1,0:T(8,128)(2,1)S(1)}, bf16[1024,512]{1,0:T(8,128)(2,1)S(1)}, bf16[1024,512]{1,0:T(8,128)(2,1)S(1)}, bf16[1024,512]{1,0:T(8,128)(2...) custom-call(f32[1024,1024]{1,0:T(8,128)} %momentum.1, bf16[1024,1024]{1,0:T(8,128)(2,1)} %gradient.1, ...), custom_call_target="tpu_custom_call" | custom-call | tf_op jit(solution)/shard_map/factors/pallas_call | solution.py:536
  88.7 5.2 %outputs.1 = (bf16[1024,1024]{1,0:T(8,128)(2,1)}, f32[1024,1024]{1,0:T(8,128)}, bf16[1024,512]{1,0:T(8,128)(2,1)}) custom-call(f32[1024,1024]{1,0:T(8,128)S(1)} %get-tuple-element.9.b, bf16[1024,1024]{1,0:T(8,128)(2,1)S(1)} %get-tuple-element.10.w, bf16[1024,512]{1,0:T(8,128)(2,1)S(1)} %get-tuple-element.11.scaled, ...), custom_call_target="tpu_custom_call" | custom-call | tf_op jit(solution)/shard_map/outputs/pallas_call | solution.py:584

commit v2 on v1

--- a/solution.py
+++ b/solution.py
@@ -54,7 +54,8 @@
     return jnp.broadcast_to(x[:, k : k + 1], (8, NB))
 
 
-HALF = NB // 16
+GROUP = 8
+NEAR = 7
 
 
 def exact(a, b, contract):
@@ -63,18 +64,20 @@
     )
 
 
-def invert_leaf(z_ref, between):
+def invert_leaf(z_ref, between, rest):
     rows = lax.broadcasted_iota(jnp.int32, (8, NB), 0)
     lanes = lax.broadcasted_iota(jnp.int32, (8, NB), 1)
     tiles = [z_ref[8 * i : 8 * i + 8, :] for i in range(NB // 8)]
     for p in range(NB // 8):
+        if rest:
+            rest.pop(0)()
         tile = tiles[p]
         columns = [from_lane(tile, 8 * p + k) for k in range(8)]
         own = (lanes >= 8 * p) & (lanes < 8 * p + 8)
         tile = jnp.where(own, jnp.where(lanes - 8 * p == rows, 1.0, 0.0), tile)
-        below = tiles[p + 1 : (p // HALF + 1) * HALF]
-        near = [from_lane(below[0], 8 * p + k) for k in range(8)] if below else None
-        upper, factors = [], []
+        below = tiles[p + 1 : (p // GROUP + 1) * GROUP]
+        near = [[from_lane(t, 8 * p + k) for k in range(8)] for t in below[:NEAR]]
+        upper, factors = [], [[] for _ in near]
         for j in range(8):
             inverse = lax.rsqrt(from_row(columns[j], j))
             t = columns[j] * inverse
@@ -82,13 +85,13 @@
             u = from_row(tile, j) * inverse
             upper.append(u)
             tile = jnp.where(rows == j, u, tile - masked * u)
-            if near:
-                factors.append(near[j] * inverse)
+            for n, f in zip(near, factors):
+                f.append(n[j] * inverse)
             for k in range(j + 1, 8):
                 tk = from_row(t, k)
                 columns[k] = columns[k] - masked * tk
-                if near:
-                    near[k] = near[k] - factors[j] * tk
+                for n, f in zip(near, factors):
+                    n[k] = n[k] - f[j] * tk
         tiles[p] = tile
 
         def eliminated(x, factors):
@@ -97,24 +100,27 @@
                 terms = [terms[i] + terms[i + 1] for i in range(0, len(terms), 2)]
             return jnp.where(own, 0.0, x) - terms[0]
 
-        if below:
-            tiles[p + 1] = eliminated(below[0], factors)
-        if len(below) > 1:
+        for i, (t, f) in enumerate(zip(below, factors)):
+            tiles[p + 1 + i] = eliminated(t, f)
+        if len(below) > NEAR:
             turned = tile.T
-            for i in range(p + 2, p + 1 + len(below)):
+            for i in range(p + 1 + NEAR, p + 1 + len(below)):
                 part = turned[8 * i : 8 * i + 8, :]
                 tiles[i] = eliminated(tiles[i], [from_lane(part, k) for k in range(8)])
-        if p == HALF - 1:
+        if p + 1 == NB // 16:
             between()
-            done = jnp.concatenate(tiles[:HALF], axis=0)
-            row = lax.broadcasted_iota(jnp.int32, done.shape, 0)
+        if (p + 1) % GROUP == 0 and p + 1 < NB // 8:
+            top, end = p + 1 - GROUP, p + 1
+            done = jnp.concatenate(tiles[top:end], axis=0)
+            row = 8 * top + lax.broadcasted_iota(jnp.int32, done.shape, 0)
             lane = lax.broadcasted_iota(jnp.int32, done.shape, 1)
-            inside = lane < 8 * HALF
-            rest = jnp.concatenate(tiles[HALF:], axis=0)
-            rest = jnp.where(inside, 0.0, rest) - exact(
-                done[:, 8 * HALF :], jnp.where(inside & (lane > row), 0.0, done), dims(0, 0)
+            inside = (lane >= 8 * top) & (lane < 8 * end)
+            later = jnp.concatenate(tiles[end:], axis=0)
+            lane2 = lax.broadcasted_iota(jnp.int32, later.shape, 1)
+            later = jnp.where((lane2 >= 8 * top) & (lane2 < 8 * end), 0.0, later) - exact(
+                done[:, 8 * end :], jnp.where(inside & (lane > row), 0.0, done), dims(0, 0)
             )
-            tiles[HALF:] = [rest[8 * i : 8 * i + 8, :] for i in range(HALF)]
+            tiles[end:] = [later[8 * i : 8 * i + 8, :] for i in range(NB // 8 - end)]
     for i in range(NB // 8):
         z_ref[8 * i : 8 * i + 8, :] = tiles[i]
 
@@ -123,21 +129,59 @@
     lower = lax.broadcasted_iota(jnp.int32, (NB, NB), 0) >= lax.broadcasted_iota(
         jnp.int32, (NB, NB), 1
     )
+    rest = []
     for b in range(R // NB):
         lo, hi = b * NB, (b + 1) * NB
         d_ref[...] = z_ref[lo:hi, lo:hi]
-        invert_leaf(d_ref, lambda: between(2 * b))
+        invert_leaf(d_ref, lambda: between(2 * b), rest)
+        while rest:
+            rest.pop(0)()
         block = jnp.where(lower, d_ref[...], 0.0)
         z_ref[lo:hi, lo:hi] = block
-        if b:
+        if hi < R:
+            follow = slice(hi, hi + NB)
+            first = exact(block, z_ref[lo:hi, follow], dims(1, 0))
+            z_ref[follow, follow] -= exact(first, first, dims(0, 0))
+            z_ref[lo:hi, follow] = first
+        rest = later_work(z_ref, lo, hi, block)
+        between(2 * b + 1)
+    while rest:
+        rest.pop(0)()
+    for b in range(R // NB - 1):
+        z_ref[b * NB : (b + 1) * NB, (b + 1) * NB :] = jnp.zeros((NB, R - (b + 1) * NB), F32)
+
+
+def later_work(z_ref, lo, hi, block):
+    parts = []
+    if lo:
+
+        def own_rows():
             z_ref[lo:hi, :lo] = exact(block, z_ref[lo:hi, :lo], dims(1, 0))
-        if hi < R:
-            upper = exact(block, z_ref[lo:hi, hi:], dims(1, 0))
-            z_ref[lo:hi, hi:] = upper
-            z_ref[hi:, lo:hi] = jnp.zeros((R - hi, NB), F32)
-            z_ref[hi:, :] -= exact(upper, z_ref[lo:hi, :], dims(0, 0))
-            z_ref[lo:hi, hi:] = jnp.zeros((NB, R - hi), F32)
-        between(2 * b + 1)
+
+        parts.append(own_rows)
+    if hi + NB < R:
+
+        def upper_rows():
+            z_ref[lo:hi, hi + NB :] = exact(block, z_ref[lo:hi, hi + NB :], dims(1, 0))
+
+        parts.append(upper_rows)
+    for i in range(hi, R, NB):
+        rows = slice(i, i + NB)
+
+        def inverse_part(rows=rows):
+            zero = jnp.zeros((NB, NB), F32)
+            before = jnp.concatenate([z_ref[rows, :lo], zero], axis=1) if lo else zero
+            z_ref[rows, :hi] = before - exact(
+                z_ref[lo:hi, rows], z_ref[lo:hi, :hi], dims(0, 0)
+            )
+
+        def upper_part(rows=rows, start=i + NB if i == hi else i):
+            z_ref[rows, start:] -= exact(z_ref[lo:hi, rows], z_ref[lo:hi, start:], dims(0, 0))
+
+        parts.append(inverse_part)
+        if i + NB < R or i > hi:
+            parts.append(upper_part)
+    return parts
 
 
 class Copies:
@@ -257,7 +301,7 @@
     part, first_a, first_b, left, far_x, near_x, far_z, near_z, far_x2, near_x2, far_z2, near_z2,
     gram, packed, packed_sum, gram_in, gram_y,
     right, right_in, right_sum, right_far, right_near,
-    tri, block, tri_h, tri_l, squares,
+    tri, block, tri_h, tri_l, squares, square_rows,
     load_sems, send_sems, recv_sems,
 ):
     r, c = lax.axis_index("row"), lax.axis_index("col")
@@ -386,13 +430,13 @@
             else:
                 gram[lo:hi, lo:] += term
 
-    def add_right(ahead, first):
+    def add_right(ahead, first, start=0, count=COLS):
         a, b = slices(ahead)
         h, l = halves(ahead)
 
-        @pl.loop(0, COLS // 256)
+        @pl.loop(0, count // 256)
         def _(k):
-            rows = pl.ds(pl.multiple_of(k * 256, 256), 256)
+            rows = pl.ds(pl.multiple_of(start + k * 256, 256), 256)
             bh = jnp.concatenate([high_t[rows, a], high_t[rows, b]], axis=1)
             bl = jnp.concatenate([low_t[rows, a], low_t[rows, b]], axis=1)
             both = dot(jnp.concatenate([bh, bl], axis=0), h)
@@ -429,11 +473,12 @@
         return pl.ds(pl.multiple_of(which * (PACKED // 2) + of * PIECE, 8), PIECE)
 
     swap_g = copies.start(packed.at[piece(1 - core, c)], gram_in, sibling)
-    add_right(2, False)
+    add_right(2, False, (1 - core) * (COLS // 2), COLS // 2)
     swaps_w = [
         copies.start(right.at[other_w, cols], right_in.at[:, cols], sibling)
         for cols in CHUNKS
     ]
+    add_right(2, False, core * (COLS // 2), COLS // 2)
     swap_g.wait_recv()
     gram_y[y] = packed[piece(core, c), :] + gram_in[...]
     over_y = [copies.start(gram_y.at[y], gram_y.at[y], at(dy=k)) for k in (2, 1, 3)]
@@ -479,7 +524,7 @@
         swap.wait_recv()
 
     tri_h[...], tri_l[...] = split(tri[...].T)
-    squares[c] = jnp.zeros((8, R), F32)
+    square_rows[...] = jnp.zeros((8, R), F32)
     h2 = R // 2
 
     def solved(value):
@@ -498,8 +543,11 @@
         rows = pl.ds(pl.multiple_of(k * 256, 256), 256)
         value = solved(right_sum[rows, :])
         mom[rows, R:] = value
-        squares[c] += jnp.sum((value * value).reshape(32, 8, R), axis=0)
-
+        square_rows[...] += jnp.sum((value * value).reshape(32, 8, R), axis=0)
+
+    row = jnp.sum(square_rows[...], axis=0, keepdims=True)
+    quarters = [row[:, i : i + NB] for i in range(0, R, NB)]
+    squares[c] = jnp.concatenate(quarters + [jnp.zeros((4, NB), F32)], axis=0)
     sums = []
     for k in range(1, 16):
         sums.append(copies.start(squares.at[c], squares.at[c], (r, lax.rem(c + k, 16))))
@@ -518,7 +566,7 @@
     total = squares[0]
     for k in range(1, 16):
         total = total + squares[k]
-    total = jnp.sum(total, axis=0, keepdims=True)
+    total = jnp.concatenate([total[i : i + 1, :] for i in range(R // NB)], axis=1)
     scale = jnp.sqrt(total / N + epsilon)
     inverse = 1.0 / scale
     right_out[...] = (mom[:, R:] * inverse).astype(BF16)
@@ -552,7 +600,7 @@
             *ring(SLICE, R), *ring(SLICE, R), *ring(SUB, R), *ring(SUB, R),
             f(R, R), f(PACKED, NB), f(PACKED, NB), f(PIECE, NB), f(4, PIECE, NB),
             f(COLS, R), f(COLS // 2, R), f(COLS, R), *ring(COLS // 8, R),
-            f(R, R), f(NB, NB), b(R, R), b(R, R), f(16, 8, R),
+            f(R, R), f(NB, NB), b(R, R), b(R, R), f(16, 8, NB), f(8, R),
             pltpu.SemaphoreType.DMA((18,)),
             pltpu.SemaphoreType.DMA((COPIES,)),
             pltpu.SemaphoreType.DMA((COPIES,)),

time: 94 us -> 92.9 us (0.988)
  Pallas kernels: 93.3 us -> 92.1 us
    pallas_call x1, Pallas kernels: 88.1 us -> 86.9 us  [factors(): pl.pallas_call(kernel, out_shape=[jax.ShapeDtypeStruct((COLS, R), BF16),...]
where the time goes in v2:
time: 92.9 us; the launch traced here: 92.8 us
  Pallas kernels  92.1 us (99%)
    pallas_call x1, Pallas kernels, factors(): pl.pallas_call(kernel, out_shape=[jax.ShapeDtypeStruct((COLS, R), BF16),...  86.9 us
    pallas_call x1, Pallas kernels, outputs(): pl.pallas_call(last_kernel, grid=(ROWS // rows,), out_shape=[jax.ShapeDty...  5.23 us

profile of v2, /device:TPU:1, one launch (start us, length us, event | category | flops | bytes accessed | tf_op | source)
XLA Modules:
  0.0 92.8 jit_solution(5991949708342491231)
XLA Ops:
  0.6 86.9 %factors.1 = (bf16[1024,512]{1,0:T(8,128)(2,1)S(1)}, bf16[1024,512]{1,0:T(8,128)(2,1)S(1)}, bf16[1024,512]{1,0:T(8,128)(2,1)S(1)}, bf16[1024,512]{1,0:T(8,128)(2...) custom-call(f32[1024,1024]{1,0:T(8,128)} %momentum.1, bf16[1024,1024]{1,0:T(8,128)(2,1)} %gradient.1, ...), custom_call_target="tpu_custom_call" | custom-call | tf_op jit(solution)/shard_map/factors/pallas_call | solution.py:584
  87.5 5.2 %outputs.1 = (bf16[1024,1024]{1,0:T(8,128)(2,1)}, f32[1024,1024]{1,0:T(8,128)}, bf16[1024,512]{1,0:T(8,128)(2,1)}) custom-call(f32[1024,1024]{1,0:T(8,128)S(1)} %get-tuple-element.9.b, bf16[1024,1024]{1,0:T(8,128)(2,1)S(1)} %get-tuple-element.10.w, bf16[1024,512]{1,0:T(8,128)(2,1)S(1)} %get-tuple-element.11.scaled, ...), custom_call_target="tpu_custom_call" | custom-call | tf_op jit(solution)/shard_map/outputs/pallas_call | solution.py:632

commit v3 on v2

--- a/solution.py
+++ b/solution.py
@@ -454,7 +454,6 @@
     add_gram(1, False)
     add_gram(3, False)
     add_right(1, False)
-    add_right(3, False)
     for a, b in outer:
         a.gather_end()
         b.gather_end()
@@ -473,15 +472,17 @@
         return pl.ds(pl.multiple_of(which * (PACKED // 2) + of * PIECE, 8), PIECE)
 
     swap_g = copies.start(packed.at[piece(1 - core, c)], gram_in, sibling)
-    add_right(2, False, (1 - core) * (COLS // 2), COLS // 2)
+    for ahead in (3, 2):
+        add_right(ahead, False, (1 - core) * (COLS // 2), COLS // 2)
     swaps_w = [
         copies.start(right.at[other_w, cols], right_in.at[:, cols], sibling)
         for cols in CHUNKS
     ]
-    add_right(2, False, core * (COLS // 2), COLS // 2)
     swap_g.wait_recv()
     gram_y[y] = packed[piece(core, c), :] + gram_in[...]
     over_y = [copies.start(gram_y.at[y], gram_y.at[y], at(dy=k)) for k in (2, 1, 3)]
+    for ahead in (3, 2):
+        add_right(ahead, False, core * (COLS // 2), COLS // 2)
     for cols, swap, ring in zip(CHUNKS, swaps_w, rings_w):
         swap.wait_recv()
         right[mine_w, cols] += right_in[:, cols]

time: 92.9 us -> 92.6 us (level)
  no operation moved by 1% of the time
where the time goes in v3:
time: 92.6 us; the launch traced here: 92.5 us
  Pallas kernels  91.9 us (99%)
    pallas_call x1, Pallas kernels, factors(): pl.pallas_call(kernel, out_shape=[jax.ShapeDtypeStruct((COLS, R), BF16),...  86.7 us
    pallas_call x1, Pallas kernels, outputs(): pl.pallas_call(last_kernel, grid=(ROWS // rows,), out_shape=[jax.ShapeDty...  5.23 us

profile of v3, /device:TPU:1, one launch (start us, length us, event | category | flops | bytes accessed | tf_op | source)
XLA Modules:
  0.0 92.5 jit_solution(18080983384229174652)
XLA Ops:
  0.6 86.7 %factors.1 = (bf16[1024,512]{1,0:T(8,128)(2,1)S(1)}, bf16[1024,512]{1,0:T(8,128)(2,1)S(1)}, bf16[1024,512]{1,0:T(8,128)(2,1)S(1)}, bf16[1024,512]{1,0:T(8,128)(2...) custom-call(f32[1024,1024]{1,0:T(8,128)} %momentum.1, bf16[1024,1024]{1,0:T(8,128)(2,1)} %gradient.1, ...), custom_call_target="tpu_custom_call" | custom-call | tf_op jit(solution)/shard_map/factors/pallas_call | solution.py:585
  87.3 5.2 %outputs.1 = (bf16[1024,1024]{1,0:T(8,128)(2,1)}, f32[1024,1024]{1,0:T(8,128)}, bf16[1024,512]{1,0:T(8,128)(2,1)}) custom-call(f32[1024,1024]{1,0:T(8,128)S(1)} %get-tuple-element.9.b, bf16[1024,1024]{1,0:T(8,128)(2,1)S(1)} %get-tuple-element.10.w, bf16[1024,512]{1,0:T(8,128)(2,1)S(1)} %get-tuple-element.11.scaled, ...), custom_call_target="tpu_custom_call" | custom-call | tf_op jit(solution)/shard_map/outputs/pallas_call | solution.py:633
